TPU v7x, 32 devices: a whole 2x2x4 slice. The times are simulated.
32 devices in a mesh: dp: 8 (over y, x, core), tensor: 4 (over z).
Axes of the slice: x: 2, y: 2, z: 4, core: 2. Of those that a mesh axis runs over, the one named last changes fastest.
Arguments:
- inputs: bfloat16 [16384, 768], P('dp'), may hold values from -6 to 6
- w_qkv: bfloat16 [768, 3, 768], P(None, None, 'tensor'), may hold values from -0.3125 to 0.3125
- b_qv: float32 [2, 768], P(None, 'tensor'), may hold values from -3 to 3
- w_out: bfloat16 [768, 768], P('tensor'), may hold values from -1.25 to 1.25
- b_out: float32 [768], replicated, may hold values from -3 to 3
- g_one: float32 [768], replicated, may hold values from 0.5 to 1.5
- s_one: float32 [768], replicated, may hold values from -3 to 3
- w_up: bfloat16 [768, 3072], P(None, 'tensor'), may hold values from -0.21875 to 0.21875
- b_up: float32 [3072], P('tensor'), may hold values from -3 to 3
- w_down: bfloat16 [3072, 768], P('tensor'), may hold values from -0.15625 to 0.15625
- b_down: float32 [768], replicated, may hold values from -3 to 3
- g_two: float32 [768], replicated, may hold values from 0.5 to 1.5
- s_two: float32 [768], replicated, may hold values from -3 to 3
- cotangent: bfloat16 [16384, 768], P('dp'), may hold values from -6 to 6
- pad_mask: int32 [16384], P('dp'), may hold values 0 or 1
- doc_lengths: int32 [32], P('dp'), may hold values from 30 to 512, as said below
Outputs:
- out: bfloat16 [16384, 768], P('dp')
- d_inputs: float32 [16384, 768], P('dp')
- d_w_qkv: float32 [768, 3, 768], P(None, None, 'tensor')
- d_b_qv: float32 [2, 768], P(None, 'tensor')
- d_w_out: float32 [768, 768], P('tensor')
- d_b_out: float32 [768], replicated
- d_g_one: float32 [768], replicated
- d_s_one: float32 [768], replicated
- d_w_up: float32 [768, 3072], P(None, 'tensor')
- d_b_up: float32 [3072], P('tensor')
- d_w_down: float32 [3072, 768], P('tensor')
- d_b_down: float32 [768], replicated
- d_g_two: float32 [768], replicated
- d_s_two: float32 [768], replicated
Inputs may be any that keep to these rules, and one draw needn't show every extreme that they name: `doc_lengths`: in every draw one document has 512 true tokens and one has 30. Rows at or beyond a document's count are padding: they are no keys whatever pad_mask says, and their outputs are zero. The first token of a document is always a key.
All inputs are finite; a program needn't handle non-finite values. No bound on the sum of `pad_mask` on one device may be relied on, other than what follows from the above.
Results may differ from a plain program's by a relative error of at most 0.014.
The roundings to bfloat16 on the way count: a program that leaves them out, or rounds other values in their place, can miss the bound.
Values may be sent and summed in bfloat16 or wider, within the bound.
No kernel may reach another device: no remote copies, remote signals or barrier semaphores. Data moves between devices by JAX's collectives and lax.ppermute only.
A program may use at most 128 MiB of HBM per device.

v0:
```python
import jax
import jax.numpy as jnp
from jax import lax
from jax.sharding import PartitionSpec as P

HD = 64


def norm_layer(values, gain, shift):
    center = values - jnp.mean(values, axis=-1, keepdims=True)
    spread = jnp.mean(center * center, axis=-1, keepdims=True)
    return center * lax.rsqrt(spread + 1e-05) * gain + shift


def gelu_exact(values):
    return jax.nn.gelu(values, approximate=False)


def masked_scores(queries, key_rows, key_valid):
    scores = jnp.einsum("qhe,khe->hqk", queries, key_rows, preferred_element_type=jnp.float32)
    return jnp.where(key_valid[None, None, :], scores, -1e30)


def doc_forward(packed):
    queries, key_rows, values, key_valid = packed
    scores = masked_scores(queries, key_rows, key_valid)
    log_total = jax.nn.logsumexp(scores, axis=-1, keepdims=True)
    weights = jnp.exp(scores - log_total).astype(jnp.bfloat16)
    context = jnp.einsum("hqk,khe->qhe", weights, values, preferred_element_type=jnp.float32)
    return (context.astype(jnp.bfloat16), log_total)


def doc_backward(packed):
    queries, key_rows, values, key_valid, log_total, d_context = packed
    scores = masked_scores(queries, key_rows, key_valid)
    weights = jnp.exp(scores - log_total)
    d_prob = jnp.einsum("qhe,khe->hqk", d_context, values, preferred_element_type=jnp.float32)
    d_values = jnp.einsum(
        "hqk,qhe->khe", weights.astype(jnp.bfloat16), d_context, preferred_element_type=jnp.float32
    )
    d_scores = (weights * (d_prob - jnp.sum(d_prob * weights, axis=-1, keepdims=True))).astype(
        jnp.bfloat16
    )
    d_query = jnp.einsum("hqk,khe->qhe", d_scores, key_rows, preferred_element_type=jnp.float32)
    d_keys = jnp.einsum("hqk,qhe->khe", d_scores, queries, preferred_element_type=jnp.float32)
    return (
        d_query.astype(jnp.bfloat16),
        d_keys.astype(jnp.bfloat16),
        d_values.astype(jnp.bfloat16),
    )


def per_device(
    inputs,
    w_qkv,
    b_qv,
    w_out,
    b_out,
    g_one,
    s_one,
    w_up,
    b_up,
    w_down,
    b_down,
    g_two,
    s_two,
    cotangent,
    pad_mask,
    doc_lengths,
):
    rows = inputs.shape[0]
    doc_count = doc_lengths.shape[0]
    length = rows // doc_count
    local_heads = w_qkv.shape[2] // HD
    scale = HD ** (-0.5)
    position = jnp.arange(length, dtype=jnp.int32)
    inside = position[None, :] < doc_lengths[:, None]
    key_valid = inside & ((pad_mask.reshape(doc_count, length) == 1) | (position[None, :] == 0))
    row_weight = inside.astype(jnp.float32).reshape(rows, 1)
    projected = jnp.einsum("td,dce->tce", inputs, w_qkv, preferred_element_type=jnp.float32)
    queries = ((projected[:, 0] + b_qv[0]) * scale).astype(jnp.bfloat16)
    key_rows = projected[:, 1].astype(jnp.bfloat16)
    values = (projected[:, 2] + b_qv[1]).astype(jnp.bfloat16)
    shaped = (doc_count, length, local_heads, HD)
    queries_doc = queries.reshape(shaped)
    keys_doc = key_rows.reshape(shaped)
    values_doc = values.reshape(shaped)
    context, log_total = lax.map(doc_forward, (queries_doc, keys_doc, values_doc, key_valid))
    context = context.reshape(rows, local_heads * HD)
    heads_part = jnp.dot(context, w_out, preferred_element_type=jnp.float32)
    attn = lax.psum(heads_part, "tensor")
    z_one = inputs.astype(jnp.float32) + attn + b_out
    h_one, pull_one = jax.vjp(norm_layer, z_one, g_one, s_one)
    h_low = h_one.astype(jnp.bfloat16)
    up_value = jnp.dot(h_low, w_up, preferred_element_type=jnp.float32) + b_up
    act, pull_act = jax.vjp(gelu_exact, up_value)
    act_low = act.astype(jnp.bfloat16)
    down_part = jnp.dot(act_low, w_down, preferred_element_type=jnp.float32)
    down = lax.psum(down_part, "tensor")
    z_two = h_one + down + b_down
    normed, pull_two = jax.vjp(norm_layer, z_two, g_two, s_two)
    d_ztwo, d_gtwo, d_stwo = pull_two(cotangent.astype(jnp.float32) * row_weight)
    d_bdown = jnp.sum(d_ztwo, axis=0)
    result = (normed * row_weight).astype(jnp.bfloat16)
    dz_two_low = d_ztwo.astype(jnp.bfloat16)
    d_wdown = jnp.einsum("tf,td->fd", act_low, dz_two_low, preferred_element_type=jnp.float32)
    d_act = jnp.einsum("td,fd->tf", dz_two_low, w_down, preferred_element_type=jnp.float32)
    d_up_low = pull_act(d_act)[0].astype(jnp.bfloat16)
    d_bup = jnp.sum(d_up_low, axis=0, dtype=jnp.float32)
    d_wup = jnp.einsum("td,tf->df", h_low, d_up_low, preferred_element_type=jnp.float32)
    hone_part = jnp.einsum("tf,df->td", d_up_low, w_up, preferred_element_type=jnp.float32)
    d_hone = lax.psum(hone_part, "tensor") + d_ztwo
    d_zone, d_gone, d_sone = pull_one(d_hone)
    d_bout = jnp.sum(d_zone, axis=0)
    dz_one_low = d_zone.astype(jnp.bfloat16)
    d_wout = jnp.einsum("th,td->hd", context, dz_one_low, preferred_element_type=jnp.float32)
    d_context = jnp.einsum(
        "td,hd->th", dz_one_low, w_out, preferred_element_type=jnp.float32
    ).astype(jnp.bfloat16)
    back_items = (
        queries_doc,
        keys_doc,
        values_doc,
        key_valid,
        log_total,
        d_context.reshape(shaped),
    )
    d_query, d_keys, d_values = lax.map(doc_backward, back_items)
    d_query = d_query.reshape(rows, local_heads * HD) * jnp.asarray(scale, jnp.bfloat16)
    stacked = jnp.stack(
        [d_query, d_keys.reshape(rows, local_heads * HD), d_values.reshape(rows, local_heads * HD)],
        axis=1,
    )
    d_wqkv = jnp.einsum("td,tce->dce", inputs, stacked, preferred_element_type=jnp.float32)
    d_bqv = jnp.stack(
        [
            jnp.sum(stacked[:, 0], axis=0, dtype=jnp.float32),
            jnp.sum(stacked[:, 2], axis=0, dtype=jnp.float32),
        ]
    )
    input_part = jnp.einsum("tce,dce->td", stacked, w_qkv, preferred_element_type=jnp.float32)
    d_inputs = lax.psum(input_part, "tensor") + d_zone
    summed = lax.psum(
        (
            d_wqkv,
            d_bqv,
            d_wout,
            d_bout,
            d_gone,
            d_sone,
            d_wup,
            d_bup,
            d_wdown,
            d_bdown,
            d_gtwo,
            d_stwo,
        ),
        "dp",
    )
    return (
        result,
        d_inputs,
        summed[0],
        summed[1],
        summed[2],
        summed[3],
        summed[4],
        summed[5],
        summed[6],
        summed[7],
        summed[8],
        summed[9],
        summed[10],
        summed[11],
    )


def solution(mesh):
    placed = (
        P("dp", None),
        P(None, None, "tensor"),
        P(None, "tensor"),
        P("tensor", None),
        P(),
        P(),
        P(),
        P(None, "tensor"),
        P("tensor"),
        P("tensor", None),
        P(),
        P(),
        P(),
        P("dp", None),
        P("dp"),
        P("dp"),
    )
    return jax.shard_map(
        per_device,
        mesh=mesh,
        in_specs=placed,
        out_specs=(
            P("dp", None),
            P("dp", None),
            P(None, None, "tensor"),
            P(None, "tensor"),
            P("tensor", None),
            P(),
            P(),
            P(),
            P(None, "tensor"),
            P("tensor"),
            P("tensor", None),
            P(),
            P(),
            P(),
        ),
        check_vma=False,
    )
```

profile of v0, /device:TPU:9, one launch (start us, length us, event | category | flops | bytes accessed | tf_op | source)
XLA Modules:
  0.0 1199.5 jit_solution(13847251560515117021)
XLA Ops:
  7.2 4.2 fusion.90
  13.5 3.1 squeeze.34
  16.6 2.2 squeeze.35
  21.1 2.9 fusion.73
  25.0 13.6 %while.26 = (s32[]{:T(128)}, bf16[4,512,3,64]{1,3,2,0:T(8,128)(2,1)}, f32[4,3,512,1]{2,1,3,0:T(4,128)}, bf16[4,512,3,64]{1,3,2,0:T(8,128)(2,1)S(1)}, pred[4,512]...) while((s32[]{:T(128)}, ...), condition=%wide.region_3.4_spmd, body=%wide.region_0.3_spmd.sunk | while | flops 207728640 | bytes 10306649 | solution.py:88
  41.7 4.7 fusion.91
  46.7 221.7 %all-reduce.8.cloned.1.call-done = f32[2048,768]{1,0:T(8,128)} async-done(((f32[2048,768]{1,0:T(8,128)}), f32[2048,768]{1,0:T(8,128)}) %all-reduce.8.cloned.1.call-update) | async-done | bytes 6291472 | tf_op jit(solution)/shard_map/psum | solution.py:91
  268.4 4.6 fusion.88
  275.7 18.3 %multiply_convert_fusion.2 = (bf16[2048,768]{1,0:T(8,128)(2,1)S(1)}, f32[2048,768]{1,0:T(8,128)}, f32[2048,768]{1,0:T(8,128)}) fusion(f32[768]{0:T(1024)S(1)} %copy-done.35, bf16[2048,768]{1,0:T(8,128)(2,1)S(1)} %fusion.69, bf16[768,768]{1,0:T(8,128)(2,1)S(1)} %copy-done), kind=kOutput, calls=%fused_computation.84 | convolution fusion | flops 2519728128 | bytes 20057088 | tf_op jit(solution)/shard_map/dot_general | solution.py:95
  295.8 4.5 fusion.92
  300.6 221.6 %all-reduce.10.cloned.1.call-done = f32[2048,768]{1,0:T(8,128)} async-done(((f32[2048,768]{1,0:T(8,128)}), f32[2048,768]{1,0:T(8,128)}) %all-reduce.10.cloned.1.call-update) | async-done | bytes 6291472 | tf_op jit(solution)/shard_map/psum | solution.py:99
  522.1 5.7 fusion.86
  529.7 3.6 multiply_reduce_fusion.1
  533.4 4.9 fusion.85
  538.3 9.3 convert_reduce_fusion
  549.3 4.5 fusion.93
  554.4 221.4 %all-reduce.12.cloned.1.call-done = f32[2048,768]{1,0:T(8,128)} async-done(((f32[2048,768]{1,0:T(8,128)}), f32[2048,768]{1,0:T(8,128)}) %all-reduce.12.cloned.1.call-update) | async-done | bytes 6291472 | tf_op jit(solution)/shard_map/psum | solution.py:112
  775.8 8.7 multiply_reduce_fusion.2
  784.5 4.3 fusion.84
  788.8 2.7 copy-done.3
  795.6 30.5 %while.27 = (s32[]{:T(128)}, bf16[4,512,3,64]{1,3,2,0:T(8,128)(2,1)S(1)}, bf16[4,512,3,64]{1,3,2,0:T(8,128)(2,1)}, bf16[4,512,3,64]{1,3,2,0:T(8,128)(2,1)S(1)}, ...) while((s32[]{:T(128)}, ...), condition=%wide.region_17.18_spmd, body=%wide.region_15.17_spmd.sunk | while | flops 513047040 | bytes 25611892 | solution.py:128
  828.3 2.1 constant_dynamic-update-slice_fusion.2
  833.0 2.3 stack_reshape.7
  837.2 7.2 convolution_bitcast_fusion
  844.5 7.1 fusion.94
  851.6 7.7 fusion.81
  862.2 3.2 fusion.75
  866.9 199.5 %all-reduce.14.cloned.1.call-done = f32[2048,768]{1,0:T(8,128)} async-done(((f32[2048,768]{1,0:T(8,128)}), f32[2048,768]{1,0:T(8,128)}) %all-reduce.14.cloned.1.call-update) | async-done | bytes 6291472 | tf_op jit(solution)/shard_map/psum | solution.py:142
  1066.3 7.7 add_reduce_fusion
  1074.0 23.4 %all-reduce = (f32[2,192]{1,0:T(2,128)}, f32[768]{0:T(1024)}, f32[768]{0:T(1024)}, f32[768]{0:T(1024)}, f32[768]{0:T(1024)}, /*index=5*/f32[768]{0:T(1024)}, f32[768]{0:T(1024)}, f32[768]{0:T(1024)}) all-reduce(f32[2,192]{1,0:T(2,128)S(1)} %pad_maximum_fusion, ...), channel_id=1, replica_groups=mesh['dp'=8,'tensor'=4] {'dp'}, use_global_device_ids=true, to_apply=%region_22.23 | all-reduce | flops 5760 | bytes 46080 | tf_op jit(solution)/shard_map/psum | solution.py:143
  1097.4 87.7 %all-reduce.16.cloned.1.call-done = (f32[768,3,192]{0,2,1:T(8,128)}, f32[192,768]{1,0:T(8,128)}, f32[768,768]{1,0:T(8,128)}, f32[768,768]{1,0:T(8,128)}) async-done(((f32[768,3,192]{0,2,1:T(8,128)}, f32[192,768]{1,0:T(8,128)}, f32[768,768]{1,0:T(8,128)}, f32[768,768]{1,0:T(8,128)}), (f32[768,3,192]{0,2,1:T(8,128)}, f32[192,768]{1,0:T(8,128)}, f32[768,768]{1,0:T(8,128)}, ...) | async-done | bytes 7077904 | tf_op jit(solution)/shard_map/psum | solution.py:143
  1185.1 2.9 copy.107
  (207 shorter events, 81.1 us)
Async XLA Ops:
  7.2 268.5 %copy-start = (bf16[768,768]{1,0:T(8,128)(2,1)S(1)}, bf16[768,768]{1,0:T(8,128)(2,1)}, u32[]{:S(2)}) copy-start(bf16[768,768]{1,0:T(8,128)(2,1)} %param.27) | copy-start | bytes 3538948
  7.2 261.2 %all-reduce.8.cloned.1.call-start = ((), (), s32[]{:S(2)}) async-start(), calls=%async_computation | async-start | bytes 12582912 | tf_op jit(solution)/shard_map/psum | solution.py:91
  11.5 7.3 copy-start.32
  12.8 7.5 copy-start.27
  38.6 7.8 copy-start.10
  41.7 226.7 %copy-start.29 = (f32[768]{0:T(1024)S(1)}, f32[768]{0:T(1024)}, u32[]{:S(2)}) copy-start(f32[768]{0:T(1024)} %param.24) | copy-start | bytes 9220
  46.4 475.7 %all-reduce.10.cloned.1.call-start = ((), (), s32[]{:S(2)}) async-start(), calls=%async_computation.1 | async-start | bytes 12582912 | tf_op jit(solution)/shard_map/psum | solution.py:99
  275.7 18.3 %copy-start.12 = (bf16[2048,768]{1,0:T(8,128)(2,1)}, bf16[2048,768]{1,0:T(8,128)(2,1)S(1)}, u32[]{:S(2)}) copy-start(bf16[2048,768]{1,0:T(8,128)(2,1)S(1)} %fusion.69) | copy-start | bytes 9437188
  275.7 20.1 %copy-start.33 = (bf16[768,768]{1,0:T(8,128)(2,1)S(1)}, bf16[768,768]{1,0:T(8,128)(2,1)}, u32[]{:S(2)}) copy-start(bf16[768,768]{1,0:T(8,128)(2,1)} %param.29) | copy-start | bytes 3538948
  300.2 221.9 %copy-start.30 = (f32[768]{0:T(1024)S(1)}, f32[768]{0:T(1024)}, u32[]{:S(2)}) copy-start(f32[768]{0:T(1024)} %param.30) | copy-start | bytes 9220
  300.2 475.5 %all-reduce.12.cloned.1.call-start = ((), (), s32[]{:S(2)}) async-start(), calls=%async_computation.2 | async-start | bytes 12582912 | tf_op jit(solution)/shard_map/psum | solution.py:112
  529.7 8.5 slice-start.2
  533.4 4.9 copy-start.34
  533.4 4.9 slice-start.3
  538.3 9.4 copy-start.4
  538.3 237.5 %copy-start.19 = (f32[2048]{0:T(1024)}, f32[2048]{0:T(1024)S(1)}, u32[]{:S(2)}) copy-start(f32[2048]{0:T(1024)S(1)} %negate_multiply_fusion.2) | copy-start | bytes 24580
  553.9 512.5 %all-reduce.14.cloned.1.call-start = ((), (), s32[]{:S(2)}) async-start(), calls=%async_computation.3 | async-start | bytes 12582912 | tf_op jit(solution)/shard_map/psum | solution.py:142
  784.5 7.0 copy-start.16
  826.1 9.2 copy-start.8
  844.4 7.1 copy-start.20
  844.4 340.6 %all-reduce.16.cloned.1.call-start = ((), (), s32[]{:S(2)}) async-start(), calls=%async_computation.4 | async-start | bytes 14155776 | tf_op jit(solution)/shard_map/psum | solution.py:143
  844.5 7.1 copy-start.38
  844.5 14.8 %slice-start = ((s8[6291456]{0:T(1024)(128)(4,1)}), s8[4194304]{0:T(1024)(128)(4,1)S(1)}, s32[]{:S(2)}) async-start(s8[6291456]{0:T(1024)(128)(4,1)} %bitcast.157), calls=%async_computation.5 | async-start | bytes 8388608
  851.5 7.7 slice-start.1
  851.6 7.7 copy-start.7
  866.8 207.2 %copy-start.21 = (f32[768]{0:T(1024)S(1)}, f32[768]{0:T(1024)}, u32[]{:S(2)}) copy-start(f32[768]{0:T(1024)} %get-tuple-element.150) | copy-start | bytes 9220
  866.8 207.2 %copy-start.24 = (f32[768]{0:T(1024)S(1)}, f32[768]{0:T(1024)}, u32[]{:S(2)}) copy-start(f32[768]{0:T(1024)} %get-tuple-element.145) | copy-start | bytes 9220
  866.8 207.2 %copy-start.25 = (f32[768]{0:T(1024)S(1)}, f32[768]{0:T(1024)}, u32[]{:S(2)}) copy-start(f32[768]{0:T(1024)} %get-tuple-element.149) | copy-start | bytes 9220
  866.8 207.1 %copy-start.26 = (f32[768]{0:T(1024)S(1)}, f32[768]{0:T(1024)}, u32[]{:S(2)}) copy-start(f32[768]{0:T(1024)} %get-tuple-element.215) | copy-start | bytes 9220
  866.9 207.1 %copy-start.28 = (f32[768]{0:T(1024)S(1)}, f32[768]{0:T(1024)}, u32[]{:S(2)}) copy-start(f32[768]{0:T(1024)} %get-tuple-element.223) | copy-start | bytes 9220
  1185.1 6.3 copy-start.14
  1185.1 7.7 copy-start.1
  (16 other events, 36.7 us)
Sparse Core Ops, SparseCore 0:
  46.5 221.8 all-reduce.7
  300.4 221.7 all-reduce.9
  554.0 221.7 all-reduce.11
  844.5 221.7 all-reduce.13
  1071.0 114.0 all-reduce.15
where the time goes:
time: 1210 us; the launch traced here: 1200 us
  waiting for transfers between devices  952 us (79%)
  matrix products  107 us (9%)
  other arithmetic  55.1 us (5%)
  local copies, waits for them, and re-layouts  46.5 us (4%)
  blocking collectives  23.4 us (2%)
  between operations  14.5 us (1%)
    psum x1, waiting for transfers between devices, per_device(): attn = lax.psum(heads_part, 'tensor')  222 us
    psum x1, waiting for transfers between devices, per_device(): down = lax.psum(down_part, 'tensor')  222 us
    psum x1, waiting for transfers between devices, per_device(): d_hone = lax.psum(hone_part, 'tensor') + d_ztwo  221 us
    psum x1, waiting for transfers between devices, per_device(): d_inputs = lax.psum(input_part, 'tensor') + d_zone  199 us
    psum x1, waiting for transfers between devices, per_device(): lax.psum((d_wqkv, d_bqv, d_wout, d_bout, d_gone, d_sone, d_wup, d_bup, d_...  87.7 us
  transfers between devices with their start and end apart: 5, of which 5 were waited for; matrix products, arithmetic and copies ran while one was open for 2% of the time, Pallas kernels for 0%

commit v1 on v0

v1 whole, which is shorter than its diff:
```python
import jax
import jax.numpy as jnp
from jax import lax
from jax.sharding import PartitionSpec as P

HD = 64
BF = jnp.bfloat16
F32 = jnp.float32


def norm_layer(values, gain, shift):
    center = values - jnp.mean(values, axis=-1, keepdims=True)
    spread = jnp.mean(center * center, axis=-1, keepdims=True)
    return center * lax.rsqrt(spread + 1e-05) * gain + shift


def gelu_exact(values):
    return jax.nn.gelu(values, approximate=False)


class Links:
    def __init__(self, n_dp, n_t):
        self.n_dp, self.n_t = n_dp, n_t
        self.bits = [1 << b for b in range(n_dp.bit_length() - 1)]
        self.orders = (self.bits[1:], self.bits[:0:-1])

    def swap(self, x, bit):
        return lax.ppermute(x, "dp", [(i, i ^ bit) for i in range(self.n_dp)])

    def shift(self, x, step):
        return lax.ppermute(x, "tensor", [((i + step) % self.n_t, i) for i in range(self.n_t)])

    def spread_plane(self, x):
        half = x.shape[1] // 2
        parts = []
        for order, part in zip(self.orders, (x[:, :half], x[:, half:])):
            slots, held = [0], part[:, None]
            for bit in order:
                held = jnp.concatenate([held, self.swap(held, bit)], axis=1)
                slots = slots + [s | bit for s in slots]
            parts.append(jnp.stack([held[:, slots.index(s)] for s in sorted(slots)], axis=1))
        even = jnp.concatenate(parts, axis=2)
        odd = self.swap(even, 1)
        pieces, _, rows, width = even.shape
        return jnp.stack([even, odd], axis=2).reshape(pieces, self.n_dp, rows, width)

    def sum_plane(self, x):
        pieces, _, rows, width = x.shape
        pairs = x.reshape(pieces, self.n_dp // 2, 2, rows, width)
        held = pairs[:, :, 0] + self.swap(pairs[:, :, 1], 1)
        half = rows // 2
        done = []
        for order, part in zip(self.orders, (held[:, :, :half], held[:, :, half:])):
            slots = list(range(0, self.n_dp, 2))
            for bit in order:
                keep = [s for s in slots if not s & bit]
                kept = jnp.stack([part[:, slots.index(s)] for s in keep], axis=1)
                sent = jnp.stack([part[:, slots.index(s | bit)] for s in keep], axis=1)
                part, slots = kept + self.swap(sent, bit), keep
            done.append(part[:, 0])
        return jnp.concatenate(done, axis=1)

    def gather_weights(self, own):
        others = jnp.stack([self.shift(own[0], k) for k in range(1, self.n_t)])
        return jnp.concatenate([own[None], self.spread_plane(others)], axis=0)

    def sum_grads(self, grads):
        mine = self.sum_plane(grads)
        total = mine[0].astype(F32)
        for k in range(1, self.n_t):
            total = total + self.shift(mine[k], self.n_t - k).astype(F32)
        return self.spread_plane(total.astype(BF)[None])[0]

    def sum_small(self, x):
        for bit in self.bits:
            x = x + self.swap(x, bit)
        bit = 1
        while bit < self.n_t:
            x = x + lax.ppermute(x, "tensor", [(i, i ^ bit) for i in range(self.n_t)])
            bit *= 2
        return x

    def reorder(self, x):
        me = lax.axis_index("dp")
        return jnp.concatenate(
            [lax.dynamic_slice_in_dim(x, me ^ s, 1, axis=0) for s in range(self.n_dp)], axis=0
        )

    def place_docs(self, own):
        me = lax.axis_index("tensor")
        rows = own.shape[0]
        whole = jnp.zeros((self.n_t * rows, own.shape[1]), own.dtype)
        for k in range(self.n_t):
            part = own if k == 0 else self.shift(own, k)
            whole = lax.dynamic_update_slice(whole, part, (((me + k) % self.n_t) * rows, 0))
        return whole


def head_scores(queries, key_rows, key_valid):
    scores = jnp.einsum("nqhe,nkhe->nhqk", queries, key_rows, preferred_element_type=F32)
    return jnp.where(key_valid[:, None, None, :], scores, -1e30)


def per_device(
    n_dp,
    n_t,
    inputs,
    w_qkv,
    b_qv,
    w_out,
    b_out,
    g_one,
    s_one,
    w_up,
    b_up,
    w_down,
    b_down,
    g_two,
    s_two,
    cotangent,
    pad_mask,
    doc_lengths,
):
    links = Links(n_dp, n_t)
    t_index = lax.axis_index("tensor")
    width = inputs.shape[1]
    length = inputs.shape[0] // doc_lengths.shape[0]
    docs = doc_lengths.shape[0] // n_t
    rows = docs * length
    heads = w_qkv.shape[2] // HD
    hidden = w_up.shape[1]
    slot_e = HD // n_dp
    slot_f = hidden // n_dp
    all_heads = heads * n_t
    scale = HD ** (-0.5)

    def own_rows(x):
        return lax.dynamic_slice_in_dim(x, t_index * rows, rows, axis=0)

    x_low = own_rows(inputs)
    d_out = own_rows(cotangent)
    lengths = lax.dynamic_slice_in_dim(doc_lengths, t_index * docs, docs)
    mask = own_rows(pad_mask).reshape(docs, length)
    position = jnp.arange(length, dtype=jnp.int32)
    inside = position[None, :] < lengths[:, None]
    key_valid = inside & ((mask == 1) | (position[None, :] == 0))
    row_weight = inside.astype(F32).reshape(rows, 1)

    w_qkv_t = w_qkv.reshape(width, 3 * heads * HD).T.reshape(3 * heads, n_dp, slot_e, width)
    w_heads = jnp.concatenate([w_qkv_t, w_out.reshape(heads, n_dp, slot_e, width)], axis=0)
    w_heads = w_heads.transpose(1, 0, 2, 3).reshape(n_dp, 4 * heads * slot_e, width)
    own_heads = links.reorder(w_heads)
    own_up = links.reorder(w_up.T.reshape(n_dp, slot_f, width))
    own_down = links.reorder(w_down.reshape(n_dp, slot_f, width))
    biases = jnp.concatenate(
        [
            links.reorder(
                b_qv.reshape(2 * heads, n_dp, slot_e).transpose(1, 0, 2).reshape(n_dp, -1)
            ),
            links.reorder(b_up.reshape(n_dp, slot_f)),
        ],
        axis=1,
    )
    biases = jnp.stack([biases] + [links.shift(biases, k) for k in range(1, n_t)])
    bias_qv = biases[:, :, : 2 * heads * slot_e].reshape(n_t, n_dp, 2, heads, slot_e)
    bias_qv = bias_qv.transpose(2, 0, 3, 1, 4).reshape(2, all_heads * HD)
    bias_up = biases[:, :, 2 * heads * slot_e :].reshape(n_t * hidden)

    all_w = links.gather_weights(own_heads).reshape(n_t, n_dp, 4, heads, slot_e, width)
    all_w = all_w.transpose(2, 0, 3, 1, 4, 5).reshape(4, all_heads * HD, width)
    all_up = links.gather_weights(own_up).reshape(n_t * hidden, width)
    all_down = links.gather_weights(own_down).reshape(n_t * hidden, width)

    def nt(a, b):
        return lax.dot_general(a, b, (((1,), (1,)), ((), ())), preferred_element_type=F32)

    def nn(a, b):
        return lax.dot_general(a, b, (((1,), (0,)), ((), ())), preferred_element_type=F32)

    def tn(a, b):
        return lax.dot_general(a, b, (((0,), (0,)), ((), ())), preferred_element_type=F32)

    shaped = (docs, length, all_heads, HD)
    queries = ((nt(x_low, all_w[0]) + bias_qv[0]) * scale).astype(BF).reshape(shaped)
    key_rows = nt(x_low, all_w[1]).astype(BF).reshape(shaped)
    values = (nt(x_low, all_w[2]) + bias_qv[1]).astype(BF).reshape(shaped)
    scores = head_scores(queries, key_rows, key_valid)
    log_total = jax.nn.logsumexp(scores, axis=-1, keepdims=True)
    prob_low = jnp.exp(scores - log_total).astype(BF)
    context = jnp.einsum("nhqk,nkhe->nqhe", prob_low, values, preferred_element_type=F32)
    context = context.astype(BF).reshape(rows, all_heads * HD)
    z_one = x_low.astype(F32) + nn(context, all_w[3]) + b_out
    h_one, pull_one = jax.vjp(norm_layer, z_one, g_one, s_one)
    h_low = h_one.astype(BF)
    up_value = nt(h_low, all_up) + bias_up
    act, pull_act = jax.vjp(gelu_exact, up_value)
    act_low = act.astype(BF)
    z_two = h_one + nn(act_low, all_down) + b_down
    normed, pull_two = jax.vjp(norm_layer, z_two, g_two, s_two)
    result = links.place_docs((normed * row_weight).astype(BF))

    d_ztwo, d_gtwo, d_stwo = pull_two(d_out.astype(F32) * row_weight)
    d_bdown = jnp.sum(d_ztwo, axis=0)
    dz_two_low = d_ztwo.astype(BF)
    d_wdown = tn(act_low, dz_two_low).astype(BF)
    d_up_low = pull_act(nt(dz_two_low, all_down))[0].astype(BF)
    d_bup = jnp.sum(d_up_low, axis=0, dtype=F32)
    d_wup = tn(d_up_low, h_low).astype(BF)
    ffn_grads = jnp.concatenate(
        [
            d_wup.reshape(n_t, n_dp, slot_f, width),
            d_wdown.reshape(n_t, n_dp, slot_f, width),
        ],
        axis=2,
    )
    ffn_sum = links.reorder(links.sum_grads(ffn_grads))
    d_hone = nn(d_up_low, all_up) + d_ztwo
    d_zone, d_gone, d_sone = pull_one(d_hone)
    d_bout = jnp.sum(d_zone, axis=0)
    dz_one_low = d_zone.astype(BF)
    d_wout = tn(context, dz_one_low).astype(BF)
    d_context = nt(dz_one_low, all_w[3]).astype(BF).reshape(shaped)

    scores = head_scores(*lax.optimization_barrier((queries, key_rows, key_valid)))
    weights = jnp.exp(scores - log_total)
    d_prob = jnp.einsum("nqhe,nkhe->nhqk", d_context, values, preferred_element_type=F32)
    d_values = jnp.einsum(
        "nhqk,nqhe->nkhe", weights.astype(BF), d_context, preferred_element_type=F32
    ).astype(BF)
    inner = jnp.sum(d_prob * weights, axis=-1, keepdims=True)
    d_scores = (weights * (d_prob - inner)).astype(BF)
    d_query = jnp.einsum("nhqk,nkhe->nqhe", d_scores, key_rows, preferred_element_type=F32)
    d_query = d_query.astype(BF) * jnp.asarray(scale, BF)
    d_keys = jnp.einsum("nhqk,nqhe->nkhe", d_scores, queries, preferred_element_type=F32)
    d_keys = d_keys.astype(BF)
    flat = (rows, all_heads * HD)
    stacked = [d_query.reshape(flat), d_keys.reshape(flat), d_values.reshape(flat)]
    d_input = nn(stacked[0], all_w[0]) + nn(stacked[1], all_w[1]) + nn(stacked[2], all_w[2])
    d_inputs = links.place_docs((d_input + d_zone).astype(BF)).astype(F32)
    head_grads = jnp.stack([tn(s, x_low).astype(BF) for s in stacked] + [d_wout])
    head_grads = head_grads.reshape(4, n_t, heads, n_dp, slot_e, width)
    head_grads = head_grads.transpose(1, 3, 0, 2, 4, 5)
    head_grads = head_grads.reshape(n_t, n_dp, 4 * heads * slot_e, width)
    head_sum = links.reorder(links.sum_grads(head_grads))

    d_bqv = jnp.stack(
        [jnp.sum(stacked[0], axis=0, dtype=F32), jnp.sum(stacked[2], axis=0, dtype=F32)]
    )
    d_bqv = d_bqv.reshape(2, n_t, heads, n_dp, slot_e).transpose(1, 3, 0, 2, 4)
    pieces = jnp.concatenate(
        [d_bqv.reshape(n_t, n_dp, -1), d_bup.reshape(n_t, n_dp, slot_f)], axis=2
    )
    pieces = jnp.concatenate(
        [links.reorder(pieces.transpose(1, 0, 2)).transpose(1, 0, 2)] * 2, axis=0
    )
    pieces = lax.dynamic_slice_in_dim(pieces, n_t - t_index, n_t, axis=0)
    common = jnp.stack([d_bout, d_gone, d_sone, d_bdown, d_gtwo, d_stwo])
    small = links.sum_small(jnp.concatenate([common.reshape(-1), pieces.reshape(-1)]))
    common = small[: common.size].reshape(common.shape)
    piece = lax.dynamic_slice_in_dim(
        small[common.size :].reshape(n_t, n_dp, -1), t_index, 1, axis=0
    )[0]
    d_bqv = piece[:, : 2 * heads * slot_e].reshape(n_dp, 2, heads, slot_e)
    d_bqv = d_bqv.transpose(1, 2, 0, 3).reshape(2, heads * HD)
    d_bup = piece[:, 2 * heads * slot_e :].reshape(hidden)

    head_sum = head_sum.reshape(n_dp, 4, heads, slot_e, width).transpose(1, 2, 0, 3, 4)
    head_sum = head_sum.reshape(4, heads * HD, width)
    d_wqkv = head_sum[:3].reshape(3 * heads * HD, width).T.astype(F32)
    return (
        result,
        d_inputs,
        d_wqkv.reshape(width, 3, heads * HD),
        d_bqv,
        head_sum[3].astype(F32),
        common[0],
        common[1],
        common[2],
        ffn_sum[:, :slot_f].reshape(hidden, width).T.astype(F32),
        d_bup,
        ffn_sum[:, slot_f:].reshape(hidden, width).astype(F32),
        common[3],
        common[4],
        common[5],
    )


def solution(mesh):
    n_dp, n_t = mesh.shape["dp"], mesh.shape["tensor"]

    def step(*args):
        return per_device(n_dp, n_t, *args)

    placed = (
        P("dp", None),
        P(None, None, "tensor"),
        P(None, "tensor"),
        P("tensor", None),
        P(),
        P(),
        P(),
        P(None, "tensor"),
        P("tensor"),
        P("tensor", None),
        P(),
        P(),
        P(),
        P("dp", None),
        P("dp"),
        P("dp"),
    )
    return jax.shard_map(
        step,
        mesh=mesh,
        in_specs=placed,
        out_specs=(
            P("dp", None),
            P("dp", None),
            P(None, None, "tensor"),
            P(None, "tensor"),
            P("tensor", None),
            P(),
            P(),
            P(),
            P(None, "tensor"),
            P("tensor"),
            P("tensor", None),
            P(),
            P(),
            P(),
        ),
        check_vma=False,
    )
```

time: 1210 us -> 526 us (0.43)
  waiting for transfers between devices: 952 us -> 208 us
  starting transfers between devices: 1.13 us -> 80.5 us
  blocking collectives: 23.4 us -> 0 us
  local copies, waits for them, and re-layouts: 46.5 us -> 68.5 us
    psum x5 -> x0, waiting for transfers between devices: 952 us -> none  [the longest x1 222 us: per_device(): attn = lax.psum(heads_part, 'tensor')]
    ppermute x0 -> x64, waiting for transfers between devices: none -> 208 us  [the longest x24 82.5 us: shift(): lax.ppermute(x, 'tensor', [((i + step) % self.n_t, i) for i in range(self...]
    ppermute x0 -> x64, starting transfers between devices: none -> 80.5 us  [the longest x38 43 us: swap(): return lax.ppermute(x, 'dp', [(i, i ^ bit) for i in range(self.n_dp)])]
    psum x1 -> x0, blocking collectives: 23.4 us -> none  [per_device(): lax.psum((d_wqkv, d_bqv, d_wout, d_bout, d_gone, d_sone, d_wup, d_bup, d_...]
    reduce_sum x4 -> x2, other arithmetic: 19.5 us -> 1.38 us  [norm_layer(): center = values - jnp.mean(values, axis=-1, keepdims=True)]
    another operation x1 -> x18, other arithmetic: 0.01 us -> 13.5 us  [the longest x10 9.38 us: spread_plane(): jnp.stack([even, odd], axis=2).reshape(pieces, self.n_dp, rows, width)]
    unnamed x94 -> x141, local copies, waits for them, and re-layouts: 21.4 us -> 29.6 us
    dot_general x39 -> x25, matrix products: 102 us -> 106 us  [the longest x6 37.5 us: nt(): lax.dot_general(a, b, (((1,), (1,)), ((), ())), preferred_element_type=F32)]
  transfers between devices with their start and end apart: 5 -> 64, of which waited for: 5 -> 27; matrix products, arithmetic and copies ran while one was open for 2% -> 20% of each run, Pallas kernels for 0% -> 0%
where the time goes in v1:
time: 526 us; the launch traced here: 520 us
  waiting for transfers between devices  208 us (40%)
  matrix products  106 us (20%)
  starting transfers between devices  80.5 us (15%)
  local copies, waits for them, and re-layouts  68.5 us (13%)
  other arithmetic  54.8 us (10%)
    ppermute x24, waiting for transfers between devices, shift(): lax.ppermute(x, 'tensor', [((i + step) % self.n_t, i) for i in range(self...  82.5 us
    ppermute x38, waiting for transfers between devices, swap(): return lax.ppermute(x, 'dp', [(i, i ^ bit) for i in range(self.n_dp)])  78.9 us
    ppermute x2, waiting for transfers between devices, sum_small(): x = x + lax.ppermute(x, 'tensor', [(i, i ^ bit) for i in range(self.n_t)])  46.7 us
    ppermute x38, starting transfers between devices, swap(): return lax.ppermute(x, 'dp', [(i, i ^ bit) for i in range(self.n_dp)])  43 us
    dot_general x6, matrix products, nt(): lax.dot_general(a, b, (((1,), (1,)), ((), ())), preferred_element_type=F32)  37.5 us
    ppermute x24, starting transfers between devices, shift(): lax.ppermute(x, 'tensor', [((i + step) % self.n_t, i) for i in range(self...  33.6 us
    unnamed x141, local copies, waits for them, and re-layouts  29.6 us
    dot_general x6, matrix products, tn(): lax.dot_general(a, b, (((0,), (0,)), ((), ())), preferred_element_type=F32)  17 us
  transfers between devices with their start and end apart: 64, of which 27 were waited for; matrix products, arithmetic and copies ran while one was open for 20% of the time, Pallas kernels for 0%

profile of v1, /device:TPU:9, one launch (start us, length us, event | category | flops | bytes accessed | tf_op | source)
XLA Modules:
  0.0 520.5 jit_solution(1561438903610185133)
XLA Ops:
  42.7 5.5 %collective-permute-done = bf16[96,768]{1,0:T(8,128)(2,1)S(1)} collective-permute-done((bf16[96,768]{1,0:T(8,128)(2,1)S(1)}, bf16[96,768]{1,0:T(8,128)(2,1)S(1)}, u32[]{:S(2)}, u32[]{:S(2)}) %collective-permute-start) | collective-permute-done | bytes 147488 | tf_op jit(solution)/shard_map/ppermute | solution.py:31
  49.5 4.1 collective-permute-done.1
  54.9 7.6 %collective-permute-done.11 = bf16[96,768]{1,0:T(8,128)(2,1)S(1)} collective-permute-done((bf16[96,768]{1,0:T(8,128)(2,1)S(1)}, bf16[96,768]{1,0:T(8,128)(2,1)S(1)}, u32[]{:S(2)}, u32[]{:S(2)}) %collective-permute-start.11) | collective-permute-done | bytes 147488 | tf_op jit(solution)/shard_map/ppermute | solution.py:31
  65.6 4.2 collective-permute-done.5
  75.8 5.3 %collective-permute-done.6 = bf16[3,2,48,768]{3,2,1,0:T(8,128)(2,1)S(1)} collective-permute-done((bf16[3,2,48,768]{3,2,1,0:T(8,128)(2,1)S(1)}, bf16[3,2,48,768]{3,2,1,0:T(8,128)(2,1)S(1)}, u32[]{:S(2)}, u32[]{:S(2)}) %collective-permute-start.6) | collective-permute-done | bytes 442400 | tf_op jit(solution)/shard_map/ppermute | solution.py:28
  83.3 10.2 %collective-permute-done.4 = bf16[3,2,48,768]{3,2,0,1:T(8,128)(2,1)S(1)} collective-permute-done((bf16[3,2,48,768]{3,2,0,1:T(8,128)(2,1)S(1)}, bf16[3,2,48,768]{3,2,0,1:T(8,128)(2,1)S(1)}, u32[]{:S(2)}, u32[]{:S(2)}) %collective-permute-start.4) | collective-permute-done | bytes 442400 | tf_op jit(solution)/shard_map/ppermute | solution.py:28
  133.1 3.6 pad_maximum_fusion.5
  141.0 7.0 %fusion.21 = bf16[12,64,512]{2,1,0:T(8,128)(2,1)S(1)} fusion(bf16[512,12,64]{0,2,1:T(8,128)(2,1)S(1)} %bitcast.297, f32[12,512,512]{1,2,0:T(8,128)} %copy-done.1, f32[12,512]{1,0:T(8,128)S(1)} %log_add_fusion, pred[512]{0:T(512)(128)(4,1)S(1)} %get-tuple-element.163), kind=kOutput, calls=%fused_computation.90 | convolution fusion | flops 412483584 | bytes 14180864 | tf_op jit(solution)/shard_map/nhqk,nkhe->nqhe/dot_general | solution.py:190
  155.2 19.5 %multiply_convert_fusion.1 = (bf16[512,3072]{1,0:T(8,128)(2,1)S(1)}, f32[512,3072]{1,0:T(8,128)}, f32[512,3072]{1,0:T(8,128)}) fusion(f32[3072]{0:T(1024)S(1)} %copy-done.33, bf16[3072,768]{1,0:T(8,128)(2,1)S(1)} %bitcast.309, f32[512,768]{1,0:T(8,128)S(1)} %get-tuple-element.147, f32[768]{0:T(1024)S(1)} %copy-done.42, f32[768]{0:T(1024)S(1)} %copy-done.37, ...), kind=kOutput, calls=%fused_computation.15 | convolution fusion | flops 2521694208 | bytes 22042624 | tf_op jit(solution)/shard_map/dot_general | solution.py:175
  179.3 4.5 convolution_convert_fusion
  183.9 8.6 %convert_reduce_fusion = (f32[3072]{0:T(1024)S(1)}, bf16[512,3072]{1,0:T(8,128)(2,1)}) fusion(f32[512,3072]{1,0:T(8,128)} %get-tuple-element.61, bf16[3072,768]{1,0:T(8,128)(2,1)S(1)} %bitcast.312, f32[512,768]{1,0:T(8,128)S(1)} %get-tuple-element.57, f32[512]{0:T(512)S(1)} %negate_multiply_fusion.2, f32[512,3072]{1,0:T(8,128)} %get-tuple-element.148, ...), kind=kOutput, calls=%fused_computation.13 | convolution fusion | flops 2443441152 | bytes 22046720 | tf_op jit(solution)/shard_map/dot_general | solution.py:175
  192.5 7.0 %convolution_convert_fusion.1 = bf16[3072,768]{1,0:T(8,128)(2,1)} fusion(bf16[512,3072]{1,0:T(8,128)(2,1)} %get-tuple-element.157, f32[512,768]{1,0:T(8,128)S(1)} %get-tuple-element.147, f32[768]{0:T(1024)S(1)} %copy-done.42, f32[768]{0:T(1024)S(1)} %copy-done.37, f32[512]{0:T(512)S(1)} %fusion.89, f32[512]{0:T(512)S(1)} %broadcast_multiply_fusion.1), kind=kOutput, calls=%fused_computation.36 | convolution fusion | flops 2420244480 | bytes 9447424 | tf_op jit(solution)/shard_map/dot_general | solution.py:181
  208.4 6.4 %fusion.27 = f32[12,512,512]{1,2,0:T(8,128)} fusion(bf16[1,512,12,64]{1,3,2,0:T(8,128)(2,1)S(1)} %bitcast.281, bf16[1,512,12,64]{1,3,2,0:T(8,128)(2,1)S(1)} %bitcast.287), kind=kOutput, calls=%fused_computation.111 | convolution fusion | flops 402653184 | bytes 14155776 | tf_op jit(solution)/shard_map/nqhe,nkhe->nhqk/dot_general | solution.py:100
  214.9 13.4 %multiply_reduce_fusion = (f32[12,512]{1,0:T(8,128)S(1)}, f32[12,512,512]{1,2,0:T(8,128)}) fusion(f32[12,512,512]{1,2,0:T(8,128)} %fusion.27, f32[12,512]{1,0:T(8,128)S(1)} %log_add_fusion, pred[512]{0:T(512)(128)(4,1)S(1)} %reduce.8, bf16[512,12,64]{0,2,1:T(8,128)(2,1)} %bitcast.327, bf16[512,12,64]{0,2,1:T(8,128)(2,1)} %bitcast.298), kind=kOutput, calls=%fused_computation.1 | convolution fusion | flops 415229952 | bytes 26788352 | tf_op jit(solution)/shard_map/nqhe,nkhe->nhqk/dot_general | solution.py:226
  228.5 3.6 convert_reduce_fusion.1
  234.0 7.0 %multiply_convert_fusion = bf16[12,512,512]{1,2,0:T(8,128)(2,1)S(1)} fusion(f32[12,512,512]{1,2,0:T(8,128)} %get-tuple-element.153, f32[12,512,512]{1,2,0:T(8,128)S(1)} %copy-done, f32[12,512]{1,0:T(8,128)S(1)} %get-tuple-element.152, f32[12,512]{1,0:T(8,128)S(1)} %log_add_fusion, pred[512]{0:T(512)(128)(4,1)S(1)} %reduce.8), kind=kLoop, calls=%fused_computation | loop fusion | flops 15728640 | bytes 31506944 | tf_op jit(solution)/shard_map/convert_element_type | solution.py:231
  256.5 3.1 fusion.16
  265.2 5.5 %collective-permute-done.46 = f32[9216]{0:T(1024)S(1)} collective-permute-done((f32[9216]{0:T(1024)S(1)}, f32[9216]{0:T(1024)S(1)}, u32[]{:S(2)}, u32[]{:S(2)}) %collective-permute-start.46) | collective-permute-done | bytes 36896 | tf_op jit(solution)/shard_map/ppermute | solution.py:28
  276.5 3.9 collective-permute-start.49
  288.7 46.7 %collective-permute-done.50 = f32[9216]{0:T(1024)S(1)} collective-permute-done((f32[9216]{0:T(1024)S(1)}, f32[9216]{0:T(1024)S(1)}, u32[]{:S(2)}, u32[]{:S(2)}) %collective-permute-start.50) | collective-permute-done | bytes 36896 | tf_op jit(solution)/shard_map/ppermute | solution.py:79
  342.6 3.4 collective-permute-start.31
  350.3 3.9 collective-permute-done.36
  354.2 3.4 collective-permute-start.28
  375.7 39.5 %collective-permute-done.28 = bf16[512,768]{1,0:T(8,128)(2,1)S(1)} collective-permute-done((bf16[512,768]{1,0:T(8,128)(2,1)}, bf16[512,768]{1,0:T(8,128)(2,1)S(1)}, u32[]{:S(2)}, u32[]{:S(2)}) %collective-permute-start.28) | collective-permute-done | bytes 786464 | tf_op jit(solution)/shard_map/ppermute | solution.py:31
  415.2 7.1 %collective-permute-start.40 = (bf16[96,768]{1,0:T(8,128)(2,1)S(1)}, bf16[96,768]{1,0:T(8,128)(2,1)S(1)}, u32[]{:S(2)}, u32[]{:S(2)}) collective-permute-start(bf16[96,768]{1,0:T(8,128)(2,1)S(1)} %get-tuple-element.88), channel_id=1, source_target_pairs={{1,0},{2,1},{3,2},{0,3},{5,4},{6,5},{7,6},{4,7},{9,8},{10,9},{11,1... | collective-permute-start | bytes 442376 | tf_op jit(solution)/shard_map/ppermute | solution.py:31
  430.0 20.7 %collective-permute-done.41 = bf16[1,1,48,768]{3,2,1,0:T(8,128)(2,1)S(1)} collective-permute-done((bf16[1,1,48,768]{3,2,1,0:T(8,128)(2,1)S(1)}, bf16[1,1,48,768]{3,2,1,0:T(8,128)(2,1)S(1)}, u32[]{:S(2)}, u32[]{:S(2)}) %collective-permute-start.41) | collective-permute-done | bytes 73760 | tf_op jit(solution)/shard_map/ppermute | solution.py:28
  456.5 4.5 collective-permute-start.45
  461.0 7.2 %collective-permute-done.55 = bf16[4,1,96,768]{3,2,0,1:T(8,128)(2,1)S(1)} collective-permute-done((bf16[4,1,96,768]{3,2,0,1:T(8,128)(2,1)S(1)}, bf16[4,1,96,768]{3,2,0,1:T(8,128)(2,1)S(1)}, u32[]{:S(2)}, u32[]{:S(2)}) %collective-permute-start.55) | collective-permute-done | bytes 589856 | tf_op jit(solution)/shard_map/ppermute | solution.py:28
  471.2 3.2 convert_element_type.215
  474.6 16.6 %collective-permute-done.57 = bf16[192,768]{1,0:T(8,128)(2,1)S(1)} collective-permute-done((bf16[192,768]{1,0:T(8,128)(2,1)S(1)}, bf16[192,768]{1,0:T(8,128)(2,1)S(1)}, u32[]{:S(2)}, u32[]{:S(2)}) %collective-permute-start.57) | collective-permute-done | bytes 294944 | tf_op jit(solution)/shard_map/ppermute | solution.py:31
  491.3 4.7 collective-permute-done.58
  503.5 5.6 %collective-permute-done.62 = bf16[1,2,96,768]{3,2,1,0:T(8,128)(2,1)S(1)} collective-permute-done((bf16[1,2,96,768]{3,2,1,0:T(8,128)(2,1)S(1)}, bf16[1,2,96,768]{3,2,1,0:T(8,128)(2,1)S(1)}, u32[]{:S(2)}, u32[]{:S(2)}) %collective-permute-start.62) | collective-permute-done | bytes 294944 | tf_op jit(solution)/shard_map/ppermute | solution.py:28
  (445 shorter events, 221.2 us)
Async XLA Ops:
  10.7 25.9 %collective-permute-start.19 = (bf16[96,768]{1,0:T(8,128)(2,1)}, bf16[96,768]{1,0:T(8,128)(2,1)}, u32[]{:S(2)}, u32[]{:S(2)}) collective-permute-start(bf16[96,768]{1,0:T(8,128)(2,1)} %get-tuple-element.82), channel_id=1, source_target_pairs={{1,0},{2,1},{3,2},{0,3},{5,4},{6,5},{7,6},{4,7},{9,8},{10,9},{11,1... | collective-permute-start | bytes 442376 | tf_op jit(solution)/shard_map/ppermute | solution.py:31
  10.7 28.5 %collective-permute-start.20 = (bf16[96,768]{1,0:T(8,128)(2,1)}, bf16[96,768]{1,0:T(8,128)(2,1)}, u32[]{:S(2)}, u32[]{:S(2)}) collective-permute-start(bf16[96,768]{1,0:T(8,128)(2,1)} %get-tuple-element.82), channel_id=1, source_target_pairs={{2,0},{3,1},{0,2},{1,3},{6,4},{7,5},{4,6},{5,7},{10,8},{11,9},{8,1... | collective-permute-start | bytes 442376 | tf_op jit(solution)/shard_map/ppermute | solution.py:31
  39.2 23.3 %collective-permute-start.11 = (bf16[96,768]{1,0:T(8,128)(2,1)S(1)}, bf16[96,768]{1,0:T(8,128)(2,1)S(1)}, u32[]{:S(2)}, u32[]{:S(2)}) collective-permute-start(bf16[96,768]{1,0:T(8,128)(2,1)S(1)} %get-tuple-element.86), channel_id=1, source_target_pairs={{1,0},{2,1},{3,2},{0,3},{5,4},{6,5},{7,6},{4,7},{9,8},{10,9},{11,1... | collective-permute-start | bytes 442376 | tf_op jit(solution)/shard_map/ppermute | solution.py:31
  39.2 24.5 %collective-permute-start.12 = (bf16[96,768]{1,0:T(8,128)(2,1)S(1)}, bf16[96,768]{1,0:T(8,128)(2,1)S(1)}, u32[]{:S(2)}, u32[]{:S(2)}) collective-permute-start(bf16[96,768]{1,0:T(8,128)(2,1)S(1)} %get-tuple-element.86), channel_id=1, source_target_pairs={{2,0},{3,1},{0,2},{1,3},{6,4},{7,5},{4,6},{5,7},{10,8},{11,9},{8,1... | collective-permute-start | bytes 442376 | tf_op jit(solution)/shard_map/ppermute | solution.py:31
  42.4 22.5 %collective-permute-start.13 = (bf16[96,768]{1,0:T(8,128)(2,1)S(1)}, bf16[96,768]{1,0:T(8,128)(2,1)S(1)}, u32[]{:S(2)}, u32[]{:S(2)}) collective-permute-start(bf16[96,768]{1,0:T(8,128)(2,1)S(1)} %get-tuple-element.86), channel_id=1, source_target_pairs={{3,0},{0,1},{1,2},{2,3},{7,4},{4,5},{5,6},{6,7},{11,8},{8,9},{9,10... | collective-permute-start | bytes 442376 | tf_op jit(solution)/shard_map/ppermute | solution.py:31
  53.6 17.5 %collective-permute-start.24 = (bf16[3,1,48,768]{3,2,1,0:T(8,128)(2,1)S(1)}, bf16[3,1,48,768]{3,2,1,0:T(8,128)(2,1)S(1)}, u32[]{:S(2)}, u32[]{:S(2)}) collective-permute-start(bf16[3,1,48,768]{3,2,1,0:T(8,128)(2,1)S(1)} %get-tuple-element.91), channel_id=1, source_target_pairs={{0,16},{4,20},{8,24},{12,28},{16,0},{20,4},{24,8},{28,12},{1,17},{... | collective-permute-start | bytes 663560 | tf_op jit(solution)/shard_map/ppermute | solution.py:28
  69.8 27.1 %collective-permute-start.23 = (bf16[3,2,48,768]{3,2,0,1:T(8,128)(2,1)S(1)}, bf16[3,2,48,768]{3,2,0,1:T(8,128)(2,1)S(1)}, u32[]{:S(2)}, u32[]{:S(2)}) collective-permute-start(bf16[3,2,48,768]{3,2,0,1:T(8,128)(2,1)S(1)} %pad_maximum_fusion.20), channel_id=1, source_target_pairs={{0,16},{4,20},{8,24},{12,28},{16,0},{20,4},{24,8},{28,12},{1,17},{... | collective-permute-start | bytes 1327112 | tf_op jit(solution)/shard_map/ppermute | solution.py:28
  71.5 25.4 %collective-permute-start.25 = (bf16[3,2,48,768]{3,2,1,0:T(8,128)(2,1)S(1)}, bf16[3,2,48,768]{3,2,1,0:T(8,128)(2,1)S(1)}, u32[]{:S(2)}, u32[]{:S(2)}) collective-permute-start(bf16[3,2,48,768]{3,2,1,0:T(8,128)(2,1)S(1)} %pad_maximum_fusion.21), channel_id=1, source_target_pairs={{0,8},{4,12},{8,0},{12,4},{16,24},{20,28},{24,16},{28,20},{1,9},{5... | collective-permute-start | bytes 1327112 | tf_op jit(solution)/shard_map/ppermute | solution.py:28
  73.6 19.9 %collective-permute-start.4 = (bf16[3,2,48,768]{3,2,0,1:T(8,128)(2,1)S(1)}, bf16[3,2,48,768]{3,2,0,1:T(8,128)(2,1)S(1)}, u32[]{:S(2)}, u32[]{:S(2)}) collective-permute-start(bf16[3,2,48,768]{3,2,0,1:T(8,128)(2,1)S(1)} %pad_maximum_fusion.14), channel_id=1, source_target_pairs={{0,16},{4,20},{8,24},{12,28},{16,0},{20,4},{24,8},{28,12},{1,17},{... | collective-permute-start | bytes 1327112 | tf_op jit(solution)/shard_map/ppermute | solution.py:28
  74.9 28.1 %collective-permute-start.15 = (bf16[3,2,48,768]{3,2,0,1:T(8,128)(2,1)S(1)}, bf16[3,2,48,768]{3,2,0,1:T(8,128)(2,1)S(1)}, u32[]{:S(2)}, u32[]{:S(2)}) collective-permute-start(bf16[3,2,48,768]{3,2,0,1:T(8,128)(2,1)S(1)} %pad_maximum_fusion.17), channel_id=1, source_target_pairs={{0,16},{4,20},{8,24},{12,28},{16,0},{20,4},{24,8},{28,12},{1,17},{... | collective-permute-start | bytes 1327112 | tf_op jit(solution)/shard_map/ppermute | solution.py:28
  81.1 19.0 %collective-permute-start.17 = (bf16[3,2,48,768]{3,2,0,1:T(8,128)(2,1)S(1)}, bf16[3,2,48,768]{3,2,0,1:T(8,128)(2,1)S(1)}, u32[]{:S(2)}, u32[]{:S(2)}) collective-permute-start(bf16[3,2,48,768]{3,2,0,1:T(8,128)(2,1)S(1)} %pad_maximum_fusion.18), channel_id=1, source_target_pairs={{0,8},{4,12},{8,0},{12,4},{16,24},{20,28},{24,16},{28,20},{1,9},{5... | collective-permute-start | bytes 1327112 | tf_op jit(solution)/shard_map/ppermute | solution.py:28
  98.3 53.0 %collective-permute-start.26 = (bf16[3,4,96,768]{3,2,1,0:T(8,128)(2,1)}, bf16[3,4,96,768]{3,2,1,0:T(8,128)(2,1)}, u32[]{:S(2)}, u32[]{:S(2)}) collective-permute-start(bf16[3,4,96,768]{3,2,1,0:T(8,128)(2,1)} %maximum_maximum_fusion.2), channel_id=1, source_target_pairs={{0,4},{4,0},{8,12},{12,8},{16,20},{20,16},{24,28},{28,24},{1,5},{5... | collective-permute-start | bytes 5308424 | tf_op jit(solution)/shard_map/ppermute | solution.py:28
  104.3 28.8 %collective-permute-start.18 = (bf16[3,4,96,768]{3,2,0,1:T(8,128)(2,1)}, bf16[3,4,96,768]{3,2,0,1:T(8,128)(2,1)}, u32[]{:S(2)}, u32[]{:S(2)}) collective-permute-start(bf16[3,4,96,768]{3,2,0,1:T(8,128)(2,1)} %maximum_maximum_fusion.1), channel_id=1, source_target_pairs={{0,4},{4,0},{8,12},{12,8},{16,20},{20,16},{24,28},{28,24},{1,5},{5... | collective-permute-start | bytes 5308424 | tf_op jit(solution)/shard_map/ppermute | solution.py:28
  255.0 81.2 %collective-permute-start.33 = (bf16[4,4,96,768]{3,2,1,0:T(8,128)(2,1)}, bf16[4,4,96,768]{3,2,1,0:T(8,128)(2,1)}, u32[]{:S(2)}, u32[]{:S(2)}) collective-permute-start(bf16[4,4,96,768]{3,2,1,0:T(8,128)(2,1)} %slice_bitcast_fusion), channel_id=1, source_target_pairs={{0,4},{4,0},{8,12},{12,8},{16,20},{20,16},{24,28},{28,24},{1,5},{5... | collective-permute-start | bytes 7077896 | tf_op jit(solution)/shard_map/ppermute | solution.py:28
  262.5 108.6 %collective-permute-start.51 = (bf16[4,4,192,768]{3,2,0,1:T(8,128)(2,1)}, bf16[4,4,192,768]{3,2,0,1:T(8,128)(2,1)}, u32[]{:S(2)}, u32[]{:S(2)}) collective-permute-start(bf16[4,4,192,768]{3,2,0,1:T(8,128)(2,1)} %bitcast.274), channel_id=1, source_target_pairs={{0,4},{4,0},{8,12},{12,8},{16,20},{20,16},{24,28},{28,24},{1,5},{5... | collective-permute-start | bytes 14155784 | tf_op jit(solution)/shard_map/ppermute | solution.py:28
  282.6 60.0 %collective-permute-start.30 = (bf16[512,768]{1,0:T(8,128)(2,1)}, bf16[512,768]{1,0:T(8,128)(2,1)}, u32[]{:S(2)}, u32[]{:S(2)}) collective-permute-start(bf16[512,768]{1,0:T(8,128)(2,1)} %get-tuple-element.155), channel_id=1, source_target_pairs={{1,0},{2,1},{3,2},{0,3},{5,4},{6,5},{7,6},{4,7},{9,8},{10,9},{11,1... | collective-permute-start | bytes 2359304 | tf_op jit(solution)/shard_map/ppermute | solution.py:31
  283.1 52.3 %collective-permute-start.50 = (f32[9216]{0:T(1024)S(1)}, f32[9216]{0:T(1024)S(1)}, u32[]{:S(2)}, u32[]{:S(2)}) collective-permute-start(f32[9216]{0:T(1024)S(1)} %add.368), channel_id=1, source_target_pairs={{0,2},{1,3},{2,0},{3,1},{4,6},{5,7},{6,4},{7,5},{8,10},{9,11},{10,... | collective-permute-start | bytes 110600 | tf_op jit(solution)/shard_map/ppermute | solution.py:79
  286.8 61.2 %collective-permute-start.27 = (bf16[512,768]{1,0:T(8,128)(2,1)}, bf16[512,768]{1,0:T(8,128)(2,1)}, u32[]{:S(2)}, u32[]{:S(2)}) collective-permute-start(bf16[512,768]{1,0:T(8,128)(2,1)} %get-tuple-element.59), channel_id=1, source_target_pairs={{1,0},{2,1},{3,2},{0,3},{5,4},{6,5},{7,6},{4,7},{9,8},{10,9},{11,1... | collective-permute-start | bytes 2359304 | tf_op jit(solution)/shard_map/ppermute | solution.py:31
  340.6 18.2 %collective-permute-start.34 = (bf16[4,2,48,768]{3,2,0,1:T(8,128)(2,1)}, bf16[4,2,48,768]{3,2,0,1:T(8,128)(2,1)}, u32[]{:S(2)}, u32[]{:S(2)}) collective-permute-start(bf16[4,2,48,768]{3,2,0,1:T(8,128)(2,1)} %pad_maximum_fusion.12), channel_id=1, source_target_pairs={{0,8},{4,12},{8,0},{12,4},{16,24},{20,28},{24,16},{28,20},{1,9},{5... | collective-permute-start | bytes 1769480 | tf_op jit(solution)/shard_map/ppermute | solution.py:28
  342.6 19.8 %collective-permute-start.31 = (bf16[512,768]{1,0:T(8,128)(2,1)}, bf16[512,768]{1,0:T(8,128)(2,1)S(1)}, u32[]{:S(2)}, u32[]{:S(2)}) collective-permute-start(bf16[512,768]{1,0:T(8,128)(2,1)} %get-tuple-element.155), channel_id=1, source_target_pairs={{2,0},{3,1},{0,2},{1,3},{6,4},{7,5},{4,6},{5,7},{10,8},{11,9},{8,1... | collective-permute-start | bytes 2359304 | tf_op jit(solution)/shard_map/ppermute | solution.py:31
  348.0 81.0 %collective-permute-start.32 = (bf16[512,768]{1,0:T(8,128)(2,1)}, bf16[512,768]{1,0:T(8,128)(2,1)S(1)}, u32[]{:S(2)}, u32[]{:S(2)}) collective-permute-start(bf16[512,768]{1,0:T(8,128)(2,1)} %get-tuple-element.155), channel_id=1, source_target_pairs={{3,0},{0,1},{1,2},{2,3},{7,4},{4,5},{5,6},{6,7},{11,8},{8,9},{9,10... | collective-permute-start | bytes 2359304 | tf_op jit(solution)/shard_map/ppermute | solution.py:31
  354.2 61.0 %collective-permute-start.28 = (bf16[512,768]{1,0:T(8,128)(2,1)}, bf16[512,768]{1,0:T(8,128)(2,1)S(1)}, u32[]{:S(2)}, u32[]{:S(2)}) collective-permute-start(bf16[512,768]{1,0:T(8,128)(2,1)} %get-tuple-element.59), channel_id=1, source_target_pairs={{2,0},{3,1},{0,2},{1,3},{6,4},{7,5},{4,6},{5,7},{10,8},{11,9},{8,1... | collective-permute-start | bytes 2359304 | tf_op jit(solution)/shard_map/ppermute | solution.py:31
  368.9 53.5 %collective-permute-start.38 = (bf16[96,768]{1,0:T(8,128)(2,1)S(1)}, bf16[96,768]{1,0:T(8,128)(2,1)S(1)}, u32[]{:S(2)}, u32[]{:S(2)}) collective-permute-start(bf16[96,768]{1,0:T(8,128)(2,1)S(1)} %get-tuple-element.87), channel_id=1, source_target_pairs={{3,0},{0,1},{1,2},{2,3},{7,4},{4,5},{5,6},{6,7},{11,8},{8,9},{9,10... | collective-permute-start | bytes 442376 | tf_op jit(solution)/shard_map/ppermute | solution.py:31
  368.9 55.9 %collective-permute-start.39 = (bf16[96,768]{1,0:T(8,128)(2,1)S(1)}, bf16[96,768]{1,0:T(8,128)(2,1)S(1)}, u32[]{:S(2)}, u32[]{:S(2)}) collective-permute-start(bf16[96,768]{1,0:T(8,128)(2,1)S(1)} %get-tuple-element.89), channel_id=1, source_target_pairs={{2,0},{3,1},{0,2},{1,3},{6,4},{7,5},{4,6},{5,7},{10,8},{11,9},{8,1... | collective-permute-start | bytes 442376 | tf_op jit(solution)/shard_map/ppermute | solution.py:31
  374.0 79.1 %collective-permute-start.54 = (bf16[4,2,96,768]{3,2,0,1:T(8,128)(2,1)S(1)}, bf16[4,2,96,768]{3,2,0,1:T(8,128)(2,1)S(1)}, u32[]{:S(2)}, u32[]{:S(2)}) collective-permute-start(bf16[4,2,96,768]{3,2,0,1:T(8,128)(2,1)S(1)} %stack.256), channel_id=1, source_target_pairs={{0,16},{4,20},{8,24},{12,28},{16,0},{20,4},{24,8},{28,12},{1,17},{... | collective-permute-start | bytes 3538952 | tf_op jit(solution)/shard_map/ppermute | solution.py:28
  422.4 31.5 %collective-permute-start.52 = (bf16[4,2,96,768]{3,2,0,1:T(8,128)(2,1)S(1)}, bf16[4,2,96,768]{3,2,0,1:T(8,128)(2,1)S(1)}, u32[]{:S(2)}, u32[]{:S(2)}) collective-permute-start(bf16[4,2,96,768]{3,2,0,1:T(8,128)(2,1)S(1)} %pad_maximum_fusion.9), channel_id=1, source_target_pairs={{0,8},{4,12},{8,0},{12,4},{16,24},{20,28},{24,16},{28,20},{1,9},{5... | collective-permute-start | bytes 3538952 | tf_op jit(solution)/shard_map/ppermute | solution.py:28
  424.8 45.4 %collective-permute-start.29 = (bf16[512,768]{1,0:T(8,128)(2,1)}, bf16[512,768]{1,0:T(8,128)(2,1)S(1)}, u32[]{:S(2)}, u32[]{:S(2)}) collective-permute-start(bf16[512,768]{1,0:T(8,128)(2,1)} %get-tuple-element.59), channel_id=1, source_target_pairs={{3,0},{0,1},{1,2},{2,3},{7,4},{4,5},{5,6},{6,7},{11,8},{8,9},{9,10... | collective-permute-start | bytes 2359304 | tf_op jit(solution)/shard_map/ppermute | solution.py:31
  427.5 23.2 %collective-permute-start.41 = (bf16[1,1,48,768]{3,2,1,0:T(8,128)(2,1)S(1)}, bf16[1,1,48,768]{3,2,1,0:T(8,128)(2,1)S(1)}, u32[]{:S(2)}, u32[]{:S(2)}) collective-permute-start(bf16[1,1,48,768]{3,2,1,0:T(8,128)(2,1)S(1)} %get-tuple-element.106), channel_id=1, source_target_pairs={{0,8},{4,12},{8,0},{12,4},{16,24},{20,28},{24,16},{28,20},{1,9},{5... | collective-permute-start | bytes 221192 | tf_op jit(solution)/shard_map/ppermute | solution.py:28
  429.1 23.0 %collective-permute-start.43 = (bf16[1,1,48,768]{3,2,1,0:T(8,128)(2,1)S(1)}, bf16[1,1,48,768]{3,2,1,0:T(8,128)(2,1)S(1)}, u32[]{:S(2)}, u32[]{:S(2)}) collective-permute-start(bf16[1,1,48,768]{3,2,1,0:T(8,128)(2,1)S(1)} %get-tuple-element.107), channel_id=1, source_target_pairs={{0,16},{4,20},{8,24},{12,28},{16,0},{20,4},{24,8},{28,12},{1,17},{... | collective-permute-start | bytes 221192 | tf_op jit(solution)/shard_map/ppermute | solution.py:28
  456.5 17.9 %collective-permute-start.45 = (bf16[1,4,96,768]{3,2,1,0:T(8,128)(2,1)S(1)}, bf16[1,4,96,768]{3,2,1,0:T(8,128)(2,1)S(1)}, u32[]{:S(2)}, u32[]{:S(2)}) collective-permute-start(bf16[1,4,96,768]{3,2,1,0:T(8,128)(2,1)S(1)} %maximum_maximum_fusion.4), channel_id=1, source_target_pairs={{0,4},{4,0},{8,12},{12,8},{16,20},{20,16},{24,28},{28,24},{1,5},{5... | collective-permute-start | bytes 1769480 | tf_op jit(solution)/shard_map/ppermute | solution.py:28
  468.5 22.7 %collective-permute-start.57 = (bf16[192,768]{1,0:T(8,128)(2,1)S(1)}, bf16[192,768]{1,0:T(8,128)(2,1)S(1)}, u32[]{:S(2)}, u32[]{:S(2)}) collective-permute-start(bf16[192,768]{1,0:T(8,128)(2,1)S(1)} %get-tuple-element.80), channel_id=1, source_target_pairs={{2,0},{3,1},{0,2},{1,3},{6,4},{7,5},{4,6},{5,7},{10,8},{11,9},{8,1... | collective-permute-start | bytes 884744 | tf_op jit(solution)/shard_map/ppermute | solution.py:31
  469.5 26.5 %collective-permute-start.58 = (bf16[192,768]{1,0:T(8,128)(2,1)S(1)}, bf16[192,768]{1,0:T(8,128)(2,1)S(1)}, u32[]{:S(2)}, u32[]{:S(2)}) collective-permute-start(bf16[192,768]{1,0:T(8,128)(2,1)S(1)} %get-tuple-element.79), channel_id=1, source_target_pairs={{1,0},{2,1},{3,2},{0,3},{5,4},{6,5},{7,6},{4,7},{9,8},{10,9},{11,1... | collective-permute-start | bytes 884744 | tf_op jit(solution)/shard_map/ppermute | solution.py:31
  (83 other events, 626.4 us)
